TPU v7x, 32 devices: a whole 2x2x4 slice. The times are simulated.
32 devices in a mesh: dom: 8 (over z, x), attr: 4 (over y, core).
Axes of the slice: x: 2, y: 2, z: 4, core: 2. Of those that a mesh axis runs over, the one named last changes fastest.
Arguments:
- records: bfloat16 [12288, 1024], P('dom', 'attr'), may hold values from -6 to 6
- owner: int32 [12288, 1], P('dom'), may hold values from 0 to 7; in each aligned block of 1536 rows (0 to 1535, 1536 to 3071, ...) at most 384 rows name the same one
- entity_means: bfloat16 [4096, 1024], P('dom', 'attr'), may hold values from -6 to 6
- noise_bits: int32 [24576, 512], P('dom'), may hold values from 0 to 8191
Outputs:
- new_means: float32 [4096, 1024], P('dom', 'attr')
- gram: float32 [1024, 1024], P(('dom', 'attr'))
Inputs may be any that keep to these rules, and one draw needn't show every extreme that they name: `owner`: among the records of one index of dom at most 384 name the same partition, and in every draw some partition is named by exactly 384 of them.
All inputs are finite; a program needn't handle non-finite values.
Results may differ from a plain program's by a relative error of at most 0.0013.
Values may be sent and summed in bfloat16 or wider, within the bound.
A program may use at most 64 MiB of HBM per device.

v0:
```python
import jax
import jax.numpy as jnp
from jax import lax
from jax.sharding import PartitionSpec as P


def posterior(raw, bits, live, width):
    uniform = (bits.astype(jnp.float32) + 0.5) / 8192.0
    noise = -jnp.log(-jnp.log(uniform))
    logits = 3.0 * jnp.tanh(raw * width ** (-0.5)) + noise
    expd = jnp.exp(logits)
    return (expd / jnp.sum(expd, axis=1, keepdims=True) * live[:, None]).astype(jnp.bfloat16)


def shards(records, owner, entity_means, noise_bits):
    dom_count = lax.axis_size("dom")
    attr_count = lax.axis_size("attr")
    rec_dev, feat_cols = records.shape
    slot_count = 2 * rec_dev
    capacity = slot_count // dom_count
    width = feat_cols * attr_count
    total_records = rec_dev * dom_count
    dest = owner[:, 0]
    onehot = (dest[:, None] == jnp.arange(dom_count, dtype=jnp.int32)[None, :]).astype(jnp.int32)
    rank = jnp.sum(jnp.cumsum(onehot, axis=0) * onehot, axis=1) - 1
    position = dest * capacity + rank
    packed = jnp.zeros((slot_count, feat_cols), jnp.bfloat16).at[position].set(records)
    flag_buf = (
        jnp.zeros((slot_count,), jnp.bfloat16).at[position].set(jnp.ones((rec_dev,), jnp.bfloat16))
    )
    arrived, arrived_flags = (
        lax.all_to_all(
            packed.reshape(dom_count, capacity, feat_cols),
            "dom",
            split_axis=0,
            concat_axis=0,
            tiled=True,
        ),
        lax.all_to_all(
            flag_buf.reshape(dom_count, capacity), "dom", split_axis=0, concat_axis=0, tiled=True
        ),
    )
    arrived = arrived.reshape(slot_count, feat_cols)
    live = arrived_flags.reshape(slot_count).astype(jnp.float32)
    raw = lax.psum(jnp.dot(arrived, entity_means.T, preferred_element_type=jnp.float32), "attr")
    weights = posterior(raw, noise_bits, live, width)
    sums_cols = jnp.dot(weights.T, arrived, preferred_element_type=jnp.float32)
    mass_col = jnp.sum(weights.astype(jnp.float32), axis=0)[:, None]
    recon = jnp.dot(weights, entity_means, preferred_element_type=jnp.float32)
    col_resid = ((arrived.astype(jnp.float32) - recon) * live[:, None]).astype(jnp.bfloat16)
    residual = lax.all_to_all(col_resid, "attr", split_axis=0, concat_axis=1, tiled=True)
    new_means = (sums_cols + 1.0 * entity_means.astype(jnp.float32)) / (mass_col + 1.0)
    term = lax.dot_general(
        residual, residual, (((0,), (0,)), ((), ())), preferred_element_type=jnp.float32
    )
    gram = lax.psum_scatter(term / total_records, ("dom", "attr"), scatter_dimension=0, tiled=True)
    return (new_means, gram)


def solution(mesh):
    in_specs = (P("dom", "attr"), P("dom", None), P("dom", "attr"), P("dom", None))
    out_specs = (P("dom", "attr"), P(("dom", "attr"), None))
    return jax.shard_map(shards, mesh=mesh, in_specs=in_specs, out_specs=out_specs, check_vma=False)
```

profile of v0, /device:TPU:0, one launch (start us, length us, event | category | flops | bytes accessed | tf_op | source)
XLA Modules:
  0.0 378.6 jit_solution(3994553369799011512)
XLA Ops:
  7.2 0.0 all-reduce.2.cloned.1.call-start
  7.2 0.7 reduce
  7.9 2.3 reduce-window.6
  10.2 0.3 slice_reduce_fusion
  10.5 0.2 reduce-window.9
  10.7 0.1 add_bitcast_fusion
  10.8 0.7 fusion.8
  11.6 8.0 %scatter_custom_fusion = bf16[3072,256]{1,0:T(8,128)(2,1)S(1)} fusion(s32[1536]{0:T(1024)S(1)} %fusion.8, bf16[1536,256]{1,0:T(8,128)(2,1)} %param.4, bf16[]{:T(256)} %constant.13.clone.1), kind=kCustom, calls=%fused_computation.11 | custom fusion | bytes 1573376 | tf_op jit(solution)/shard_map/scatter | solution.py:27
  19.6 44.1 %all_to_all.34 = bf16[8,384,256]{2,1,0:T(8,128)(2,1)S(1)} all-to-all(bf16[8,384,256]{2,1,0:T(8,128)(2,1)S(1)} %bitcast.34), channel_id=1, replica_groups=mesh['dom'=8,'attr'=4] {'dom'}, dimensions={0} | all-to-all | bytes 3145728 | tf_op jit(solution)/shard_map/all_to_all | solution.py:32
  63.6 4.6 %fusion.12 = f32[3072,512]{1,0:T(8,128)} fusion(bf16[3072,256]{1,0:T(8,128)(2,1)S(1)} %bitcast.31, bf16[512,256]{1,0:T(8,128)(2,1)} %param.6), kind=kOutput, calls=%fused_computation.28 | convolution fusion | flops 805306368 | bytes 8126464 | tf_op jit(solution)/shard_map/dot_general | solution.py:45
  68.3 0.0 all-reduce.2.cloned.1.call-update
  68.3 0.0 reduce-scatter.2.cloned.1.call-start
  68.3 11.1 %scatter_custom_fusion.1 = bf16[3072]{0:T(1024)(128)(2,1)S(1)} fusion(s32[1536]{0:T(1024)S(1)} %fusion.8, bf16[1536]{0:T(1024)(128)(2,1)S(1)} %broadcast.48, bf16[]{:T(256)} %constant.13.clone.1), kind=kCustom, calls=%fused_computation.24 | custom fusion | bytes 6146 | tf_op jit(solution)/shard_map/scatter | solution.py:29
  79.5 0.5 broadcast.58
  80.0 0.7 reduce.6
  80.7 0.1 reshape.84
  80.7 9.9 %all_to_all.35 = bf16[8,2,192]{2,1,0:T(2,128)(2,1)S(1)} all-to-all(bf16[8,2,192]{2,1,0:T(2,128)(2,1)S(1)} %reshape.84), channel_id=1, replica_groups=mesh['dom'=8,'attr'=4] {'dom'}, dimensions={0} | all-to-all | bytes 12288 | tf_op jit(solution)/shard_map/all_to_all | solution.py:39
  90.6 0.1 reshape.85
  90.7 96.3 %all-reduce.2.cloned.1.call-done = f32[3072,512]{1,0:T(8,128)} async-done(((f32[3072,512]{1,0:T(8,128)}), f32[3072,512]{1,0:T(8,128)}) %all-reduce.2.cloned.1.call-update) | async-done | bytes 6291472 | tf_op jit(solution)/shard_map/psum | solution.py:45
  187.0 0.0 copy-start
  187.0 7.5 %fusion.11 = f32[3072]{0:T(1024)S(1)} fusion(s32[3072,512]{1,0:T(8,128)} %param.7, f32[3072,512]{1,0:T(8,128)} %all-reduce.2.cloned.1.call-done), kind=kLoop, calls=%fused_computation.27 | loop fusion | flops 14152704 | bytes 12595200 | tf_op jit(solution)/shard_map/reduce_sum | solution.py:12
  194.6 0.0 copy-done
  194.6 0.0 copy-start.2
  194.6 5.9 %convert_reduce_fusion = (f32[512]{0:T(512)S(1)}, bf16[3072,512]{1,0:T(8,128)(2,1)S(1)}) fusion(f32[3072]{0:T(1024)S(1)} %bitcast.38, f32[3072]{0:T(1024)S(1)} %fusion.11, s32[3072,512]{1,0:T(8,128)} %param.7, f32[3072,512]{1,0:T(8,128)S(1)} %copy-done), kind=kLoop, calls=%fused_computation.2 | loop fusion | flops 20446720 | bytes 15755264 | tf_op jit(solution)/shard_map/reduce_sum | solution.py:48
  200.5 0.0 copy-start.1
  200.5 0.0 copy-done.2
  200.5 2.2 fusion.1
  202.7 0.0 copy-done.1
  202.7 1.7 copy.8
  204.4 22.5 %all_to_all.36 = bf16[4,768,256]{1,2,0:T(8,128)(2,1)S(1)} all-to-all(bf16[4,768,256]{1,2,0:T(8,128)(2,1)S(1)} %copy.8), channel_id=1, replica_groups=mesh['dom'=8,'attr'=4] {'attr'}, dimensions={0} | all-to-all | bytes 3145728 | tf_op jit(solution)/shard_map/all_to_all | solution.py:51
  226.9 3.8 convolution_multiply_fusion
  230.7 0.0 reduce-scatter.2.cloned.1.call-update
  230.7 3.7 fusion.2
  234.4 137.3 %reduce-scatter.2.cloned.1.call-done = f32[32,1024]{1,0:T(8,128)} async-done(((f32[1024,1024]{1,0:T(8,128)}), f32[32,1024]{1,0:T(8,128)}) %reduce-scatter.2.cloned.1.call-update) | async-done | bytes 131088 | tf_op jit(solution)/shard_map/reduce_scatter | solution.py:56
  (7 shorter events, 0.1 us)
Async XLA Ops:
  7.2 179.9 %all-reduce.2.cloned.1.call-start = ((), (), s32[]{:S(2)}) async-start(), calls=%async_computation.4 | async-start | bytes 12582912 | tf_op jit(solution)/shard_map/psum | solution.py:45
  68.3 303.4 %reduce-scatter.2.cloned.1.call-start = ((), (), s32[]{:S(2)}) async-start(), calls=%async_computation.5 | async-start | bytes 4325376 | tf_op jit(solution)/shard_map/reduce_scatter | solution.py:56
  187.0 7.5 %copy-start = (f32[3072,512]{1,0:T(8,128)S(1)}, f32[3072,512]{1,0:T(8,128)}, u32[]{:S(2)}) copy-start(f32[3072,512]{1,0:T(8,128)} %all-reduce.2.cloned.1.call-done) | copy-start | bytes 18874372
  194.6 5.9 %copy-start.2 = (bf16[512,256]{1,0:T(8,128)(2,1)S(1)}, bf16[512,256]{1,0:T(8,128)(2,1)}, u32[]{:S(2)}) copy-start(bf16[512,256]{1,0:T(8,128)(2,1)} %param.6) | copy-start | bytes 786436
  200.5 2.2 copy-start.1
Sparse Core Ops, SparseCore 0:
  68.4 118.5 all-reduce.1
  230.8 140.8 reduce-scatter.1
where the time goes:
time: 379 us
  waiting for transfers between devices  234 us (62%)
  blocking collectives  76.5 us (20%)
  local copies, waits for them, and re-layouts  21.8 us (6%)
  other arithmetic  18.1 us (5%)
  matrix products  14.2 us (4%)
  between operations  14.2 us (4%)
    reduce_scatter x1, waiting for transfers between devices, shards(): lax.psum_scatter(term / total_records, ('dom', 'attr'), scatter_dimension...  137 us
    psum x1, waiting for transfers between devices, shards(): lax.psum(jnp.dot(arrived, entity_means.T, preferred_element_type=jnp.floa...  96.3 us
    all_to_all x1, blocking collectives, shards(): lax.all_to_all(packed.reshape(dom_count, capacity, feat_cols), 'dom', spl...  44.1 us
    all_to_all x1, blocking collectives, shards(): lax.all_to_all(col_resid, 'attr', split_axis=0, concat_axis=1, tiled=True)  22.5 us
    scatter x1, local copies, waits for them, and re-layouts, shards(): jnp.zeros((slot_count,), jnp.bfloat16).at[position]  11.1 us
    all_to_all x1, blocking collectives, shards(): lax.all_to_all(flag_buf.reshape(dom_count, capacity), 'dom', split_axis=0...  9.89 us
    scatter x1, local copies, waits for them, and re-layouts, shards(): jnp.zeros((slot_count, feat_cols), jnp.bfloat16).at[position].set(records)  8.02 us
  transfers between devices with their start and end apart: 2, of which 2 were waited for; matrix products, arithmetic and copies ran while one was open for 4% of the time, Pallas kernels for 0%

commit v1 on v0

--- a/solution.py
+++ b/solution.py
@@ -42,7 +42,8 @@
     )
     arrived = arrived.reshape(slot_count, feat_cols)
     live = arrived_flags.reshape(slot_count).astype(jnp.float32)
-    raw = lax.psum(jnp.dot(arrived, entity_means.T, preferred_element_type=jnp.float32), "attr")
+    w_in = jnp.dot(arrived, entity_means.T, preferred_element_type=jnp.float32)
+    raw = lax.all_gather(w_in, "attr").sum(axis=0)
     weights = posterior(raw, noise_bits, live, width)
     sums_cols = jnp.dot(weights.T, arrived, preferred_element_type=jnp.float32)
     mass_col = jnp.sum(weights.astype(jnp.float32), axis=0)[:, None]

time: 379 us -> 428 us (1.13)
  waiting for transfers between devices: 234 us -> 269 us
  other arithmetic: 18.1 us -> 31.5 us
    all_gather x0 -> x1, waiting for transfers between devices: none -> 132 us  [shards(): raw = lax.all_gather(w_in, 'attr').sum(axis=0)]
    psum x1 -> x0, waiting for transfers between devices: 96.3 us -> none  [shards(): lax.psum(jnp.dot(arrived, entity_means.T, preferred_element_type=jnp.floa...]
    reduce_sum x0 -> x1, other arithmetic: none -> 13.1 us  [shards(): raw = lax.all_gather(w_in, 'attr').sum(axis=0)]
where the time goes in v1:
time: 428 us; the launch traced here: 427 us
  waiting for transfers between devices  269 us (63%)
  blocking collectives  76.5 us (18%)
  other arithmetic  31.5 us (7%)
  local copies, waits for them, and re-layouts  21.8 us (5%)
  matrix products  14.3 us (3%)
  between operations  14.2 us (3%)
    reduce_scatter x1, waiting for transfers between devices, shards(): lax.psum_scatter(term / total_records, ('dom', 'attr'), scatter_dimension...  138 us
    all_gather x1, waiting for transfers between devices, shards(): raw = lax.all_gather(w_in, 'attr').sum(axis=0)  132 us
    all_to_all x1, blocking collectives, shards(): lax.all_to_all(packed.reshape(dom_count, capacity, feat_cols), 'dom', spl...  44.1 us
    all_to_all x1, blocking collectives, shards(): lax.all_to_all(col_resid, 'attr', split_axis=0, concat_axis=1, tiled=True)  22.5 us
    reduce_sum x1, other arithmetic, shards(): raw = lax.all_gather(w_in, 'attr').sum(axis=0)  13.1 us
    scatter x1, local copies, waits for them, and re-layouts, shards(): jnp.zeros((slot_count,), jnp.bfloat16).at[position]  11.1 us
    all_to_all x1, blocking collectives, shards(): lax.all_to_all(flag_buf.reshape(dom_count, capacity), 'dom', split_axis=0...  9.89 us
  transfers between devices with their start and end apart: 2, of which 2 were waited for; matrix products, arithmetic and copies ran while one was open for 4% of the time, Pallas kernels for 0%

profile of v1, /device:TPU:0, one launch (start us, length us, event | category | flops | bytes accessed | tf_op | source)
XLA Modules:
  0.0 427.5 jit_solution(13028503721538253854)
XLA Ops:
  7.2 0.0 all-gather.3.cloned.1.call-start
  7.2 0.7 reduce
  7.9 2.3 reduce-window.6
  10.2 0.3 slice_reduce_fusion
  10.5 0.2 reduce-window.9
  10.7 0.1 add_bitcast_fusion
  10.8 0.7 fusion.8
  11.6 8.0 %scatter_custom_fusion = bf16[3072,256]{1,0:T(8,128)(2,1)S(1)} fusion(s32[1536]{0:T(1024)S(1)} %fusion.8, bf16[1536,256]{1,0:T(8,128)(2,1)} %param.4, bf16[]{:T(256)} %constant.13.clone.1), kind=kCustom, calls=%fused_computation.11 | custom fusion | bytes 1573376 | tf_op jit(solution)/shard_map/scatter | solution.py:27
  19.6 44.1 %all_to_all.34 = bf16[8,384,256]{2,1,0:T(8,128)(2,1)S(1)} all-to-all(bf16[8,384,256]{2,1,0:T(8,128)(2,1)S(1)} %bitcast.36), channel_id=1, replica_groups=mesh['dom'=8,'attr'=4] {'dom'}, dimensions={0} | all-to-all | bytes 3145728 | tf_op jit(solution)/shard_map/all_to_all | solution.py:32
  63.6 4.7 %fusion.12 = f32[3072,512]{1,0:T(8,128)} fusion(bf16[3072,256]{1,0:T(8,128)(2,1)S(1)} %bitcast.33, bf16[512,256]{1,0:T(8,128)(2,1)} %param.6), kind=kOutput, calls=%fused_computation.28 | convolution fusion | flops 805306368 | bytes 8126464 | tf_op jit(solution)/shard_map/dot_general | solution.py:45
  68.3 0.0 all-gather.3.cloned.1.call-update
  68.3 0.0 reduce-scatter.2.cloned.1.call-start
  68.4 11.1 %scatter_custom_fusion.1 = bf16[3072]{0:T(1024)(128)(2,1)S(1)} fusion(s32[1536]{0:T(1024)S(1)} %fusion.8, bf16[1536]{0:T(1024)(128)(2,1)S(1)} %broadcast.48, bf16[]{:T(256)} %constant.13.clone.1), kind=kCustom, calls=%fused_computation.24 | custom fusion | bytes 6146 | tf_op jit(solution)/shard_map/scatter | solution.py:29
  79.5 0.5 broadcast.58
  80.0 0.7 reduce.6
  80.7 0.1 reshape.85
  80.8 9.9 %all_to_all.35 = bf16[8,2,192]{2,1,0:T(2,128)(2,1)S(1)} all-to-all(bf16[8,2,192]{2,1,0:T(2,128)(2,1)S(1)} %reshape.85), channel_id=1, replica_groups=mesh['dom'=8,'attr'=4] {'dom'}, dimensions={0} | all-to-all | bytes 12288 | tf_op jit(solution)/shard_map/all_to_all | solution.py:39
  90.7 0.1 reshape.86
  90.8 131.5 %all-gather.3.cloned.1.call-done = f32[12288,512]{1,0:T(8,128)} async-done(((f32[3072,512]{1,0:T(8,128)}), f32[12288,512]{1,0:T(8,128)}) %all-gather.3.cloned.1.call-update) | async-done | bytes 25165840 | tf_op jit(solution)/shard_map/all_gather | solution.py:46
  222.3 13.1 %reduce_sum.37 = f32[3072,512]{1,0:T(8,128)} reduce(f32[4,3072,512]{2,1,0:T(8,128)} %bitcast.32, f32[]{:T(128)} %constant.8.clone.1), dimensions={0}, to_apply=%region_4.5 | reduce | flops 4718592 | bytes 31457284 | tf_op jit(solution)/shard_map/reduce_sum | solution.py:46
  235.4 0.0 copy-start
  235.4 7.8 %fusion.11 = f32[3072]{0:T(1024)S(1)} fusion(s32[3072,512]{1,0:T(8,128)} %param.7, f32[3072,512]{1,0:T(8,128)} %reduce_sum.37), kind=kLoop, calls=%fused_computation.27 | loop fusion | flops 14152704 | bytes 12595200 | tf_op jit(solution)/shard_map/reduce_sum | solution.py:12
  243.2 0.0 copy-done
  243.2 0.0 copy-start.2
  243.2 5.9 %convert_reduce_fusion = (f32[512]{0:T(512)S(1)}, bf16[3072,512]{1,0:T(8,128)(2,1)S(1)}) fusion(f32[3072]{0:T(1024)S(1)} %bitcast.40, f32[3072]{0:T(1024)S(1)} %fusion.11, s32[3072,512]{1,0:T(8,128)} %param.7, f32[3072,512]{1,0:T(8,128)S(1)} %copy-done), kind=kLoop, calls=%fused_computation.2 | loop fusion | flops 20446720 | bytes 15755264 | tf_op jit(solution)/shard_map/reduce_sum | solution.py:49
  249.1 0.0 copy-start.1
  249.1 0.0 copy-done.2
  249.2 2.2 fusion.1
  251.3 0.0 copy-done.1
  251.3 1.7 copy.8
  253.0 22.5 %all_to_all.36 = bf16[4,768,256]{1,2,0:T(8,128)(2,1)S(1)} all-to-all(bf16[4,768,256]{1,2,0:T(8,128)(2,1)S(1)} %copy.8), channel_id=1, replica_groups=mesh['dom'=8,'attr'=4] {'attr'}, dimensions={0} | all-to-all | bytes 3145728 | tf_op jit(solution)/shard_map/all_to_all | solution.py:52
  275.6 3.7 convolution_multiply_fusion
  279.3 0.0 reduce-scatter.2.cloned.1.call-update
  279.4 3.7 fusion.2
  283.1 137.6 %reduce-scatter.2.cloned.1.call-done = f32[32,1024]{1,0:T(8,128)} async-done(((f32[1024,1024]{1,0:T(8,128)}), f32[32,1024]{1,0:T(8,128)}) %reduce-scatter.2.cloned.1.call-update) | async-done | bytes 131088 | tf_op jit(solution)/shard_map/reduce_scatter | solution.py:57
  (7 shorter events, 0.1 us)
Async XLA Ops:
  7.2 215.2 %all-gather.3.cloned.1.call-start = ((), (), s32[]{:S(2)}) async-start(), calls=%async_computation.5 | async-start | bytes 31457280 | tf_op jit(solution)/shard_map/all_gather | solution.py:46
  68.3 352.3 %reduce-scatter.2.cloned.1.call-start = ((), (), s32[]{:S(2)}) async-start(), calls=%async_computation.4 | async-start | bytes 4325376 | tf_op jit(solution)/shard_map/reduce_scatter | solution.py:57
  235.4 7.8 %copy-start = (f32[3072,512]{1,0:T(8,128)S(1)}, f32[3072,512]{1,0:T(8,128)}, u32[]{:S(2)}) copy-start(f32[3072,512]{1,0:T(8,128)} %reduce_sum.37) | copy-start | bytes 18874372
  243.2 5.9 %copy-start.2 = (bf16[512,256]{1,0:T(8,128)(2,1)S(1)}, bf16[512,256]{1,0:T(8,128)(2,1)}, u32[]{:S(2)}) copy-start(bf16[512,256]{1,0:T(8,128)(2,1)} %param.6) | copy-start | bytes 786436
  249.1 2.2 copy-start.1
Sparse Core Ops, SparseCore 0:
  68.5 153.8 all-gather.2
  279.5 141.1 reduce-scatter.1
